TPU v7x, 256 devices: a whole 4x4x8 slice. The times are simulated.
256 devices in a mesh: row: 16 (over z, core), col: 16 (over x, y).
Axes of the slice: x: 4, y: 4, z: 8, core: 2. Of those that a mesh axis runs over, the one named last changes fastest.
Arguments:
- gen_showers: bfloat16 [16384, 6480], P(('row', 'col')), may hold values from -10 to 10
- ref_showers: bfloat16 [16384, 6480], P(('row', 'col')), may hold values from -10 to 10
- w_in: bfloat16 [6480, 512], replicated, may hold values from -0.078125 to 0.078125
- b_in: float32 [512], replicated, may hold values from -4 to 4
- w_out: bfloat16 [512, 256], replicated, may hold values from -0.25 to 0.25
Outputs:
- gen_potential: float32 [16384], P('row')
- ref_potential: float32 [16, 1024], P(None, 'col')
All inputs are finite; a program needn't handle non-finite values.
Results may differ from a plain program's by a relative error of at most 0.0003.
Values sent between devices are 32-bit elements; how exact they have to be, the bound alone decides.
A program may use at most 128 MiB of HBM per device.

v0:
```python
import math

import jax
import jax.numpy as jnp
from jax import lax
from jax.sharding import PartitionSpec as P

ITERS = 3


EPSILON = 0.1


def embed(showers, w_in, b_in, w_out):
    hidden = jnp.dot(showers, w_in, preferred_element_type=jnp.float32) + b_in
    hidden = jnp.maximum(hidden, 0.0)
    features = jnp.dot(hidden, w_out.astype(jnp.float32), precision=lax.Precision.HIGHEST)
    squares = jnp.sum(jnp.square(features), axis=1)
    return (features, squares)


def reduce_cols(scaled):
    largest = lax.pmax(jnp.max(scaled, axis=1), "col")
    totals = lax.psum(jnp.sum(jnp.exp(scaled - largest[:, None]), axis=1), "col")
    return -EPSILON * (largest + jnp.log(totals))


def reduce_rows(scaled):
    largest = lax.pmax(jnp.max(scaled, axis=0), "row")
    totals = lax.psum(jnp.sum(jnp.exp(scaled - largest[None, :]), axis=0), "row")
    return -EPSILON * (largest + jnp.log(totals))


def body(gen_showers, ref_showers, w_in, b_in, w_out):
    gen_feat, gen_sq = embed(gen_showers, w_in, b_in, w_out)
    ref_feat, ref_sq = embed(ref_showers, w_in, b_in, w_out)
    row_count = lax.axis_size("row")
    col_count = lax.axis_size("col")
    per_dev = gen_feat.shape[0]
    width = gen_feat.shape[1]
    gen_rows, gen_norms = (
        lax.all_gather(gen_feat, "col", axis=0, tiled=True),
        lax.all_gather(gen_sq, "col", axis=0, tiled=True),
    )
    ref_cols, ref_norms = (
        lax.all_gather(ref_feat, "row", axis=0, tiled=True),
        lax.all_gather(ref_sq, "row", axis=0, tiled=True),
    )
    total_count = row_count * col_count * per_dev
    log_weight = -math.log(total_count)

    def tile_cost():
        inner_prod = lax.dot_general(
            gen_rows,
            ref_cols,
            (((1,), (1,)), ((), ())),
            precision=lax.Precision.HIGHEST,
            preferred_element_type=jnp.float32,
        )
        return (gen_norms[:, None] + ref_norms[None, :] - 2.0 * inner_prod) / width

    ref_pot = jnp.zeros((ref_cols.shape[0],), jnp.float32)
    gen_pot = jnp.zeros((gen_rows.shape[0],), jnp.float32)
    for sweep_idx in range(ITERS):
        scaled = log_weight + (ref_pot[None, :] - tile_cost()) / EPSILON
        gen_pot = reduce_cols(scaled)
        scaled = log_weight + (gen_pot[:, None] - tile_cost()) / EPSILON
        ref_pot = reduce_rows(scaled)
    return (gen_pot, ref_pot.reshape(row_count, per_dev))


def solution(mesh):
    return jax.shard_map(
        body,
        mesh=mesh,
        in_specs=(P(("row", "col"), None), P(("row", "col"), None), P(), P(), P()),
        out_specs=(P("row"), P(None, "col")),
        check_vma=False,
    )
```

profile of v0, /device:TPU:1, one launch (start us, length us, event | category | flops | bytes accessed | tf_op | source)
XLA Modules:
  0.0 517.0 jit_solution(4666240185190480455)
XLA Ops:
  7.3 1.1 copy-done
  8.4 4.1 fusion.7
  12.6 1.0 multiply_reduce_fusion.1
  13.7 4.1 fusion.6
  17.8 1.0 multiply_reduce_fusion
  21.8 34.3 %all-reduce = f32[1024]{0:T(1024)S(1)} all-reduce(f32[1024]{0:T(1024)S(1)} %dynamic-update-slice), channel_id=1, replica_groups=mesh['row'=16,'col'=16] {'col'}, use_global_device_ids=true, to_apply=%add | all-reduce | flops 1024 | bytes 8192
  56.1 34.0 %all-reduce.1 = f32[1024]{0:T(1024)S(1)} all-reduce(f32[1024]{0:T(1024)S(1)} %dynamic-update-slice.1), channel_id=1, replica_groups=mesh['row'=16,'col'=16] {'row'}, use_global_device_ids=true, to_apply=%add.1 | all-reduce | flops 1024 | bytes 8192
  90.2 14.9 %all-gather.5.cloned.1.call-done = f32[1024,256]{1,0:T(8,128)} async-done(((f32[64,256]{1,0:T(8,128)}), f32[1024,256]{1,0:T(8,128)}) %all-gather.5.cloned.1.call-update) | async-done | bytes 1048592 | tf_op jit(solution)/shard_map/all_gather | solution.py:46
  105.1 7.9 %fusion = (f32[1024]{0:T(1024)S(1)}, f32[1024,1024]{1,0:T(8,128)}) fusion(f32[1024,256]{1,0:T(8,128)} %all-gather.3.cloned.1.call-done, f32[1024,256]{1,0:T(8,128)} %all-gather.5.cloned.1.call-done, f32[1024]{0:T(1024)S(1)} %all-reduce.1, f32[1024]{0:T(1024)S(1)} %all-reduce), kind=kOutput, calls=%fused_computation.13 | convolution fusion | flops 3229613056 | bytes 6303744 | tf_op jit(solution)/shard_map/dot_general | solution.py:53
  113.0 33.2 %pmax.42 = f32[1024]{0:T(1024)S(1)} all-reduce(f32[1024]{0:T(1024)S(1)} %get-tuple-element.6), channel_id=1, replica_groups=mesh['row'=16,'col'=16] {'col'}, use_global_device_ids=true, to_apply=%region_3.0 | all-reduce | flops 1024 | bytes 8192 | tf_op jit(solution)/shard_map/pmax | solution.py:23
  146.2 3.3 exponential_reduce_fusion.5
  149.5 28.5 %psum.42 = f32[1024]{0:T(1024)S(1)} all-reduce(f32[1024]{0:T(1024)S(1)} %exponential_reduce_fusion.5), channel_id=1, replica_groups=mesh['row'=16,'col'=16] {'col'}, use_global_device_ids=true, to_apply=%region_5.0 | all-reduce | flops 1024 | bytes 8192 | tf_op jit(solution)/shard_map/psum | solution.py:24
  178.0 2.8 fusion.1
  180.8 37.2 %pmax.43 = f32[1024]{0:T(1024)S(1)} all-reduce(f32[1024]{0:T(1024)S(1)} %fusion.1), channel_id=1, replica_groups=mesh['row'=16,'col'=16] {'row'}, use_global_device_ids=true, to_apply=%region_7.0 | all-reduce | flops 1024 | bytes 8192 | tf_op jit(solution)/shard_map/pmax | solution.py:29
  218.1 3.2 exponential_reduce_fusion.4
  221.3 23.6 %psum.43 = f32[1024]{0:T(1024)S(1)} all-reduce(f32[1024]{0:T(1024)S(1)} %exponential_reduce_fusion.4), channel_id=1, replica_groups=mesh['row'=16,'col'=16] {'row'}, use_global_device_ids=true, to_apply=%region_9.0 | all-reduce | flops 1024 | bytes 8192 | tf_op jit(solution)/shard_map/psum | solution.py:30
  244.8 2.8 fusion.2
  247.7 30.4 %pmax.44 = f32[1024]{0:T(1024)S(1)} all-reduce(f32[1024]{0:T(1024)S(1)} %fusion.2), channel_id=1, replica_groups=mesh['row'=16,'col'=16] {'col'}, use_global_device_ids=true, to_apply=%region_11.0 | all-reduce | flops 1024 | bytes 8192 | tf_op jit(solution)/shard_map/pmax | solution.py:23
  278.1 3.3 exponential_reduce_fusion.3
  281.4 28.5 %psum.44 = f32[1024]{0:T(1024)S(1)} all-reduce(f32[1024]{0:T(1024)S(1)} %exponential_reduce_fusion.3), channel_id=1, replica_groups=mesh['row'=16,'col'=16] {'col'}, use_global_device_ids=true, to_apply=%region_13.0 | all-reduce | flops 1024 | bytes 8192 | tf_op jit(solution)/shard_map/psum | solution.py:24
  309.9 2.8 fusion.3
  312.7 37.7 %pmax.45 = f32[1024]{0:T(1024)S(1)} all-reduce(f32[1024]{0:T(1024)S(1)} %fusion.3), channel_id=1, replica_groups=mesh['row'=16,'col'=16] {'row'}, use_global_device_ids=true, to_apply=%region_15.0 | all-reduce | flops 1024 | bytes 8192 | tf_op jit(solution)/shard_map/pmax | solution.py:29
  350.4 3.2 exponential_reduce_fusion.2
  353.7 23.6 %psum.45 = f32[1024]{0:T(1024)S(1)} all-reduce(f32[1024]{0:T(1024)S(1)} %exponential_reduce_fusion.2), channel_id=1, replica_groups=mesh['row'=16,'col'=16] {'row'}, use_global_device_ids=true, to_apply=%region_17.0 | all-reduce | flops 1024 | bytes 8192 | tf_op jit(solution)/shard_map/psum | solution.py:30
  377.2 2.8 fusion.4
  380.0 30.2 %pmax.46 = f32[1024]{0:T(1024)S(1)} all-reduce(f32[1024]{0:T(1024)S(1)} %fusion.4), channel_id=1, replica_groups=mesh['row'=16,'col'=16] {'col'}, use_global_device_ids=true, to_apply=%region_19.0 | all-reduce | flops 1024 | bytes 8192 | tf_op jit(solution)/shard_map/pmax | solution.py:23
  410.3 3.3 exponential_reduce_fusion.1
  413.6 28.5 %psum.46 = f32[1024]{0:T(1024)S(1)} all-reduce(f32[1024]{0:T(1024)S(1)} %exponential_reduce_fusion.1), channel_id=1, replica_groups=mesh['row'=16,'col'=16] {'col'}, use_global_device_ids=true, to_apply=%region_21.0 | all-reduce | flops 1024 | bytes 8192 | tf_op jit(solution)/shard_map/psum | solution.py:24
  442.1 2.8 fusion.5
  444.9 37.8 %pmax.47 = f32[1024]{0:T(1024)S(1)} all-reduce(f32[1024]{0:T(1024)S(1)} %fusion.5), channel_id=1, replica_groups=mesh['row'=16,'col'=16] {'row'}, use_global_device_ids=true, to_apply=%region_23.0 | all-reduce | flops 1024 | bytes 8192 | tf_op jit(solution)/shard_map/pmax | solution.py:29
  482.7 3.2 exponential_reduce_fusion
  485.9 23.6 %psum.47 = f32[1024]{0:T(1024)S(1)} all-reduce(f32[1024]{0:T(1024)S(1)} %exponential_reduce_fusion), channel_id=1, replica_groups=mesh['row'=16,'col'=16] {'row'}, use_global_device_ids=true, to_apply=%region_25.0 | all-reduce | flops 1024 | bytes 8192 | tf_op jit(solution)/shard_map/psum | solution.py:30
  (31 shorter events, 2.5 us)
Async XLA Ops:
  7.2 1.2 copy-start
  7.2 6.5 %copy-start.4 = (f32[512]{0:T(512)S(1)}, f32[512]{0:T(512)}, u32[]{:S(2)}) copy-start(f32[512]{0:T(512)} %param.8) | copy-start | bytes 6148
  7.2 5.4 %copy-start.2 = (bf16[512,256]{1,0:T(8,128)(2,1)S(1)}, bf16[512,256]{1,0:T(8,128)(2,1)}, u32[]{:S(2)}) copy-start(bf16[512,256]{1,0:T(8,128)(2,1)} %param.9) | copy-start | bytes 786436
  7.2 6.5 %copy-start.1 = (bf16[64,6480]{1,0:T(8,128)(2,1)S(1)}, bf16[64,6480]{1,0:T(8,128)(2,1)}, u32[]{:S(2)}) copy-start(bf16[64,6480]{1,0:T(8,128)(2,1)} %param.6) | copy-start | bytes 2488324
  7.2 82.9 %all-gather.3.cloned.1.call-start = ((), (), s32[]{:S(2)}) async-start(), calls=%async_computation | async-start | bytes 1114112 | tf_op jit(solution)/shard_map/all_gather | solution.py:42
  13.6 5.3 %copy-start.6 = (u32[256]{0:T(256)S(1)}, u32[256]{0:T(256)}, u32[]{:S(2)}) copy-start(u32[256]{0:T(256)} %constant.32) | copy-start | bytes 3076
  13.6 5.9 %copy-start.5 = (u32[256]{0:T(256)S(1)}, u32[256]{0:T(256)}, u32[]{:S(2)}) copy-start(u32[256]{0:T(256)} %constant.27) | copy-start | bytes 3076
  13.6 91.5 %all-gather.5.cloned.1.call-start = ((), (), s32[]{:S(2)}) async-start(), calls=%async_computation.1 | async-start | bytes 1114112 | tf_op jit(solution)/shard_map/all_gather | solution.py:46
  442.1 43.8 %copy-start.3 = (f32[1024]{0:T(1024)}, f32[1024]{0:T(1024)S(1)}, u32[]{:S(2)}) copy-start(f32[1024]{0:T(1024)S(1)} %add_multiply_fusion.1) | copy-start | bytes 12292
Sparse Core Ops, SparseCore 0:
  13.7 49.8 all-gather.2
  65.4 39.5 all-gather.4
where the time goes:
time: 518 us; the launch traced here: 517 us
  blocking collectives  431 us (83%)
  other arithmetic  33.6 us (6%)
  matrix products  18.2 us (4%)
  between operations  15.5 us (3%)
  waiting for transfers between devices  15 us (3%)
    pmax x3, blocking collectives, reduce_rows(): largest = lax.pmax(jnp.max(scaled, axis=0), 'row')  113 us
    pmax x3, blocking collectives, reduce_cols(): largest = lax.pmax(jnp.max(scaled, axis=1), 'col')  93.9 us
    psum x3, blocking collectives, reduce_cols(): lax.psum(jnp.sum(jnp.exp(scaled - largest[:, None]), axis=1), 'col')  85.5 us
    psum x3, blocking collectives, reduce_rows(): lax.psum(jnp.sum(jnp.exp(scaled - largest[None, :]), axis=0), 'row')  70.7 us
    unnamed x2, blocking collectives  68.3 us
    all_gather x1, waiting for transfers between devices, body(): lax.all_gather(ref_feat, 'row', axis=0, tiled=True)  14.9 us
  transfers between devices with their start and end apart: 2, of which 1 were waited for; matrix products, arithmetic and copies ran while one was open for 1% of the time, Pallas kernels for 0%

commit v1 on v0

v1 whole, which is shorter than its diff:
```python
import functools
import math

import jax
import jax.numpy as jnp
from jax import lax
from jax.experimental import pallas as pl
from jax.experimental.pallas import tpu as pltpu
from jax.sharding import PartitionSpec as P

EPSILON = 0.1
MESH = pl.DeviceIdType.MESH
F32 = jnp.float32
BF16 = jnp.bfloat16
LANES = 128
K_CHUNK = 1280


def split2(v):
    hi = v.astype(BF16)
    lo = (v - hi.astype(F32)).astype(BF16)
    return hi, lo


def mm(a, b):
    return jnp.dot(a, b, preferred_element_type=F32)


def kernel(
    n_row,
    n_col,
    gx,
    rx,
    w,
    b,
    wo,
    g_out,
    f_out,
    x_v,
    w_v,
    b_v,
    wo_v,
    gf,
    rf,
    g_hi,
    g_lo,
    r_hi,
    r_lo,
    tile,
    part,
    part2,
    colv,
    sqg,
    sqr,
    send1,
    recv1g,
    recv1f,
    send2,
    recv2,
    x_sem,
    w_sem,
    s_sem,
    gsend,
    grecv,
    esend,
    erecv,
):
    my_r = lax.axis_index("row")
    my_c = lax.axis_index("col")
    per = gx.shape[0]
    vox = gx.shape[1]
    feat = wo.shape[1]
    rows = per * n_col
    cols = per * n_row
    rq = rows // LANES
    cq = cols // LANES
    total = n_row * n_col * per
    kappa = 1.0 / (EPSILON * math.log(2.0))
    log2w = -math.log2(total)

    def row_peer(d):
        return (lax.rem(my_r + d, n_row), my_c)

    def col_peer(d):
        return (my_r, lax.rem(my_c + d, n_col))

    loads = [
        pltpu.make_async_copy(gx, x_v.at[pl.ds(0, per)], x_sem.at[0]),
        pltpu.make_async_copy(rx, x_v.at[pl.ds(per, per)], x_sem.at[1]),
        pltpu.make_async_copy(b, b_v, s_sem.at[0]),
        pltpu.make_async_copy(wo, wo_v, s_sem.at[1]),
    ]
    bounds = list(range(0, vox, K_CHUNK)) + [vox]
    if bounds[-1] - bounds[-2] < K_CHUNK // 2 and len(bounds) > 2:
        del bounds[-2]
    spans = list(zip(bounds[:-1], bounds[1:]))
    wloads = [
        pltpu.make_async_copy(w.at[pl.ds(k0, k1 - k0)], w_v.at[pl.ds(k0, k1 - k0)], w_sem.at[n])
        for n, (k0, k1) in enumerate(spans)
    ]
    loads[0].start()
    loads[1].start()
    for cp in wloads:
        cp.start()
    loads[2].start()
    loads[3].start()

    barrier = pltpu.get_barrier_semaphore()
    for d in range(1, n_row):
        pl.semaphore_signal(barrier, inc=1, device_id=row_peer(d), device_id_type=MESH)
    for d in range(1, n_col):
        pl.semaphore_signal(barrier, inc=1, device_id=col_peer(d), device_id_type=MESH)

    loads[0].wait()
    loads[1].wait()
    acc = None
    for n, (k0, k1) in enumerate(spans):
        wloads[n].wait()
        t = mm(x_v[:, k0:k1], w_v[k0:k1, :])
        acc = t if acc is None else acc + t
    loads[2].wait()
    loads[3].wait()
    hidden = jnp.maximum(acc + b_v[...], 0.0)
    h0 = hidden.astype(BF16)
    h1f = hidden - h0.astype(F32)
    h1 = h1f.astype(BF16)
    h2 = (h1f - h1.astype(F32)).astype(BF16)
    wov = wo_v[...]
    feats = mm(h0, wov) + (mm(h1, wov) + mm(h2, wov))
    gf[my_c] = feats[:per]
    rf[my_r] = feats[per:]

    pl.semaphore_wait(barrier, n_row + n_col - 2)

    gather = []
    for d in range(1, n_row):
        gather.append(
            pltpu.make_async_remote_copy(
                rf.at[my_r], rf.at[my_r], gsend.at[0], grecv.at[0], device_id=row_peer(d), device_id_type=MESH
            )
        )
    for d in range(1, n_col):
        gather.append(
            pltpu.make_async_remote_copy(
                gf.at[my_c], gf.at[my_c], gsend.at[1], grecv.at[1], device_id=col_peer(d), device_id_type=MESH
            )
        )
    for cp in gather:
        cp.start()

    def all_bytes(ref, count, sem):
        view = ref.at[pl.ds(0, count)]
        return pltpu.make_async_copy(view, view, sem)

    all_bytes(rf, n_row - 1, grecv.at[0]).wait()
    all_bytes(gf, n_col - 1, grecv.at[1]).wait()

    scale = 2.0 * kappa / feat
    half = cq

    for q in range(rq):
        per_q = LANES // per
        v = jnp.concatenate([gf[q * per_q + k] for k in range(per_q)], axis=0)
        hi, lo = split2(v * scale)
        g_hi[pl.ds(q * LANES, LANES), :] = hi
        g_lo[pl.ds(q * LANES, LANES), :] = lo
    for q in range(cq):
        v = jnp.concatenate([rf[q], rf[q + half]], axis=0)
        vt = v.T
        sqr[pl.ds(q, 1), :] = jnp.sum(vt * vt, axis=0, keepdims=True) * (1.0 / feat)
        hi, lo = split2(vt)
        r_hi[:, pl.ds(q * LANES, LANES)] = hi
        r_lo[:, pl.ds(q * LANES, LANES)] = lo

    nt = 256

    def tile_step(n, _):
        off = pl.multiple_of(n * nt, nt)
        rh = r_hi[:, pl.ds(off, nt)]
        rl = r_lo[:, pl.ds(off, nt)]
        gh = g_hi[...]
        tile[:, pl.ds(off, nt)] = mm(gh, rh) + (mm(g_lo[...], rh) + mm(gh, rl))
        return 0

    lax.fori_loop(0, cols // nt, tile_step, 0)

    RB = 32

    def blocks(body):
        def step(n, _):
            body(pl.multiple_of(n * RB, RB))
            return 0

        lax.fori_loop(0, rows // RB, step, 0)

    def lane_groups(v):
        return [v[:, q * LANES : (q + 1) * LANES] for q in range(cq)]

    def to_dense(src, dst, row0, op):
        for q in range(rq):
            blk = src[pl.ds(q * LANES, LANES), :].T
            dst[pl.ds(row0 + q, 1), :] = op(blk, axis=0, keepdims=True)

    def to_col(x8):
        for q in range(rq):
            colv[pl.ds(q * LANES, LANES), :] = jnp.broadcast_to(x8[q : q + 1, :], (LANES, LANES)).T

    def wide(x8, n):
        return [jnp.broadcast_to(x8[q : q + 1, :], (n, LANES)) for q in range(cq)]

    def tree(op, vs):
        vs = list(vs)
        while len(vs) > 1:
            vs = [op(vs[k], vs[k + 1]) if k + 1 < len(vs) else vs[k] for k in range(0, len(vs), 2)]
        return vs[0]

    add = lambda p, q: p + q

    def exchange(n, src, dst, me, peer, count):
        dst[me] = src[...]
        cps = [
            pltpu.make_async_remote_copy(
                src, dst.at[me], esend.at[n], erecv.at[n], device_id=peer(d), device_id_type=MESH
            )
            for d in range(1, count)
        ]
        for cp in cps:
            cp.start()
        all_bytes(dst, count - 1, erecv.at[n]).wait()
        return cps

    sent = list(gather)

    phi0 = -kappa * sqr[...] + log2w
    ph = wide(phi0, RB)

    def gen_max(off):
        t = lane_groups(tile[pl.ds(off, RB), :])
        m = tree(jnp.maximum, [a + p for a, p in zip(t, ph)])
        part[pl.ds(off, RB), :] = jnp.broadcast_to(jnp.max(m, axis=1, keepdims=True), (RB, LANES))

    blocks(gen_max)

    def gen_sum(off):
        m = part[pl.ds(off, RB), :]
        t = lane_groups(tile[pl.ds(off, RB), :])
        part2[pl.ds(off, RB), :] = tree(add, [jnp.exp2((a + p) - m) for a, p in zip(t, ph)])

    blocks(gen_sum)
    to_dense(part, send1, 0, jnp.max)
    to_dense(part2, send1, rq, jnp.sum)
    sent += exchange(0, send1, recv1g, my_c, col_peer, n_col)

    def lse2(ref, count, q):
        ms = [ref[k, 0:q, :] for k in range(count)]
        m = tree(jnp.maximum, ms)
        s = tree(add, [ref[k, q:, :] * jnp.exp2(ms[k] - m) for k in range(count)])
        return m + jnp.log2(s)

    gamma = -lse2(recv1g, n_col, rq)
    to_col(gamma + log2w)

    def ref_max(n, ms):
        off = pl.multiple_of(n * RB, RB)
        c = colv[pl.ds(off, RB), :]
        out = []
        for q in range(cq):
            t = tile[pl.ds(off, RB), q * LANES : (q + 1) * LANES] + c
            tile[pl.ds(off, RB), q * LANES : (q + 1) * LANES] = t
            out.append(jnp.maximum(ms[q], tree(jnp.maximum, [t[8 * k : 8 * k + 8] for k in range(RB // 8)])))
        return tuple(out)

    low = jnp.full((8, LANES), -jnp.inf, F32)
    ms = lax.fori_loop(0, rows // RB, ref_max, tuple(low for _ in range(cq)))
    cm = [jnp.max(m, axis=0, keepdims=True) for m in ms]
    cmb = [jnp.broadcast_to(m, (RB, LANES)) for m in cm]

    def fold(v):
        return tree(add, [v[8 * k : 8 * k + 8] for k in range(RB // 8)])

    def ref_sum(n, ss):
        off = pl.multiple_of(n * RB, RB)
        out = []
        for q in range(cq):
            e = jnp.exp2(tile[pl.ds(off, RB), q * LANES : (q + 1) * LANES] - cmb[q])
            tile[pl.ds(off, RB), q * LANES : (q + 1) * LANES] = e
            out.append(ss[q] + fold(e))
        return tuple(out)

    zero = jnp.zeros((8, LANES), F32)
    ss = lax.fori_loop(0, rows // RB, ref_sum, tuple(zero for _ in range(cq)))
    for q in range(cq):
        send2[pl.ds(q, 1), :] = cm[q]
        send2[pl.ds(cq + q, 1), :] = jnp.sum(ss[q], axis=0, keepdims=True)
    sent += exchange(1, send2, recv1f, my_r, row_peer, n_row)
    phi = -lse2(recv1f, n_row, cq)
    w8 = jnp.exp2(send2[0:cq, :] + phi)

    def gen_pass(n, scale8):
        vw = wide(scale8, RB)

        def body(off):
            t = lane_groups(tile[pl.ds(off, RB), :])
            part[pl.ds(off, RB), :] = tree(add, [a * p for a, p in zip(t, vw)])

        blocks(body)
        src = send1.at[pl.ds(0, rq)] if n == 2 else send1.at[pl.ds(rq, rq)]
        to_dense(part, send1, 0 if n == 2 else rq, jnp.sum)
        cps = exchange(n, src, recv2.at[n - 2], my_c, col_peer, n_col)
        return tree(add, [recv2[n - 2, k] for k in range(n_col)]), cps

    def ref_pass(n, scale8):
        to_col(scale8)

        def step(k, ss):
            off = pl.multiple_of(k * RB, RB)
            c = colv[pl.ds(off, RB), :]
            return tuple(
                ss[q] + fold(tile[pl.ds(off, RB), q * LANES : (q + 1) * LANES] * c) for q in range(cq)
            )

        ss = lax.fori_loop(0, rows // RB, step, tuple(zero for _ in range(cq)))
        row0 = 0 if n == 3 else cq
        for q in range(cq):
            send2[pl.ds(row0 + q, 1), :] = w8[q : q + 1, :] * jnp.sum(ss[q], axis=0, keepdims=True)
        cps = exchange(n, send2.at[pl.ds(row0, cq)], recv2.at[n - 2], my_r, row_peer, n_row)
        return tree(add, [recv2[n - 2, k] for k in range(n_row)]), cps

    def drain(n, ref, count):
        all_bytes(ref, count, esend.at[n]).wait()

    drain(0, recv1g, n_col - 1)
    r, cps = gen_pass(2, w8)
    drain(1, recv1f, n_row - 1)
    c, cps = ref_pass(3, 1.0 / r)
    r, cps = gen_pass(4, w8 / c)
    for q in range(rq):
        per_q = LANES // per
        v = jnp.concatenate([gf[q * per_q + k] for k in range(per_q)], axis=0)
        v = v * v
        s = functools.reduce(add, [v[:, k * LANES : (k + 1) * LANES] for k in range(feat // LANES)])
        sqg[pl.ds(q, 1), :] = jnp.sum(s.T, axis=0, keepdims=True) * (1.0 / feat)
    g_out[...] = (gamma - jnp.log2(r)) * (1.0 / kappa) + sqg[...]
    c, cps = ref_pass(5, 1.0 / r)
    f = (phi - jnp.log2(c)) * (1.0 / kappa) + sqr[...]
    f_out[pl.ds(0, half), :] = f[:, :per]
    f_out[pl.ds(half, half), :] = f[:, per:]
    for n, count in ((2, n_col), (3, n_row), (4, n_col), (5, n_row)):
        drain(n, recv2.at[n - 2], count - 1)
    all_bytes(rf, n_row - 1, gsend.at[0]).wait()
    all_bytes(gf, n_col - 1, gsend.at[1]).wait()


def body(n_row, n_col, gx, rx, w, b, wo):
    per, vox = gx.shape
    units, feat = wo.shape
    rows, cols = per * n_col, per * n_row
    rq, cq = rows // LANES, cols // LANES
    hbm = pl.BlockSpec(memory_space=pl.ANY)
    vmem = pl.BlockSpec(memory_space=pltpu.VMEM)
    dma = pltpu.SemaphoreType.DMA
    n_chunks = max(1, vox // K_CHUNK + 1)
    g8, f2 = pl.pallas_call(
        functools.partial(kernel, n_row, n_col),
        out_shape=(jax.ShapeDtypeStruct((rq, LANES), F32), jax.ShapeDtypeStruct((n_row, per), F32)),
        in_specs=[hbm] * 5,
        out_specs=(vmem, vmem),
        scratch_shapes=[
            pltpu.VMEM((2 * per, vox), BF16),
            pltpu.VMEM((vox, units), BF16),
            pltpu.VMEM((1, units), F32),
            pltpu.VMEM((units, feat), BF16),
            pltpu.VMEM((n_col, per, feat), F32),
            pltpu.VMEM((n_row, per, feat), F32),
            pltpu.VMEM((rows, feat), BF16),
            pltpu.VMEM((rows, feat), BF16),
            pltpu.VMEM((feat, cols), BF16),
            pltpu.VMEM((feat, cols), BF16),
            pltpu.VMEM((rows, cols), F32),
            pltpu.VMEM((rows, LANES), F32),
            pltpu.VMEM((rows, LANES), F32),
            pltpu.VMEM((rows, LANES), F32),
            pltpu.VMEM((rq, LANES), F32),
            pltpu.VMEM((cq, LANES), F32),
            pltpu.VMEM((2 * rq, LANES), F32),
            pltpu.VMEM((n_col, 2 * rq, LANES), F32),
            pltpu.VMEM((n_row, 2 * cq, LANES), F32),
            pltpu.VMEM((2 * cq, LANES), F32),
            pltpu.VMEM((4, max(n_col, n_row), max(rq, cq), LANES), F32),
            dma((2,)),
            dma((n_chunks,)),
            dma((2,)),
            dma((2,)),
            dma((2,)),
            dma((6,)),
            dma((6,)),
        ],
        compiler_params=pltpu.CompilerParams(
            collective_id=0, has_side_effects=True, vmem_limit_bytes=60 * 1024 * 1024
        ),
    )(gx, rx, w, b.reshape(1, units), wo)
    return g8.reshape(rows), f2


def solution(mesh):
    n_row, n_col = mesh.shape["row"], mesh.shape["col"]
    return jax.shard_map(
        functools.partial(body, n_row, n_col),
        mesh=mesh,
        in_specs=(P(("row", "col"), None), P(("row", "col"), None), P(), P(), P()),
        out_specs=(P("row"), P(None, "col")),
        check_vma=False,
    )
```

time: 518 us -> 83.3 us (0.16)
  blocking collectives: 431 us -> 0 us
  Pallas kernels: 0 us -> 79.9 us
  other arithmetic: 33.6 us -> 0 us
  matrix products: 18.2 us -> 0 us
  waiting for transfers between devices: 15 us -> 0 us
  between operations: 15.5 us -> 0.64 us
    pmax x6 -> x0, blocking collectives: 207 us -> none  [the longest x3 113 us: reduce_rows(): largest = lax.pmax(jnp.max(scaled, axis=0), 'row')]
    psum x6 -> x0, blocking collectives: 156 us -> none  [the longest x3 85.5 us: reduce_cols(): lax.psum(jnp.sum(jnp.exp(scaled - largest[:, None]), axis=1), 'col')]
    pallas_call x0 -> x1, Pallas kernels: none -> 79.9 us  [body(): pl.pallas_call(functools.partial(kernel, n_row, n_col), out_shape=(jax.Sh...]
    unnamed x2 -> x0, blocking collectives: 68.3 us -> none
    reduce_sum x6 -> x0, other arithmetic: 19.5 us -> none  [the longest x3 9.87 us: reduce_cols(): jnp.sum(jnp.exp(scaled - largest[:, None]), axis=1)]
    dot_general x5 -> x0, matrix products: 18.2 us -> none  [the longest x2 8.29 us: embed(): hidden = jnp.dot(showers, w_in, preferred_element_type=jnp.float32) + b_in]
    all_gather x2 -> x0, waiting for transfers between devices: 14.9 us -> none  [the longest x1 14.9 us: body(): lax.all_gather(ref_feat, 'row', axis=0, tiled=True)]
    reduce_max x5 -> x0, other arithmetic: 14 us -> none  [the longest x3 8.41 us: reduce_rows(): largest = lax.pmax(jnp.max(scaled, axis=0), 'row')]
  transfers between devices with their start and end apart: 2 -> 0, of which waited for: 1 -> 0; matrix products, arithmetic and copies ran while one was open for 1% -> 0% of each run, Pallas kernels for 0% -> 0%
where the time goes in v1:
time: 83.3 us; the launch traced here: 83.1 us
  Pallas kernels  79.9 us (96%)
  local copies, waits for them, and re-layouts  2.56 us (3%)
    pallas_call x1, Pallas kernels, body(): pl.pallas_call(functools.partial(kernel, n_row, n_col), out_shape=(jax.Sh...  79.9 us
    unnamed x2, local copies, waits for them, and re-layouts  2.56 us

profile of v1, /device:TPU:1, one launch (start us, length us, event | category | flops | bytes accessed | tf_op | source)
XLA Modules:
  0.0 83.1 jit_solution(14279121435971124836)
XLA Ops:
  0.6 79.9 %shard_map.68 = (f32[8,128]{1,0:T(8,128)}, f32[16,64]{1,0:T(8,128)}) custom-call(bf16[64,6480]{1,0:T(8,128)(2,1)} %gx.1, bf16[64,6480]{1,0:T(8,128)(2,1)} %rx.1, bf16[6480,512]{1,0:T(8,128)(2,1)} %w.1, f32[1,512]{1,0:T(1,128)} %bitcast.3, bf16[512,256]{1,0:T(8,128)(2,1)} %wo.1), custom_call_target="tpu_custom_call" | custom-call | tf_op jit(solution)/shard_map/pallas_call | solution.py:363
  80.5 1.3 %copy.9 = f32[1024]{0:T(1024)} copy(f32[1024]{0:T(1024)} %bitcast.2) | data formatting | bytes 8192
  81.8 1.3 %copy.10 = f32[16,64]{1,0:T(8,128)} copy(f32[16,64]{1,0:T(8,128)} %get-tuple-element.9) | data formatting | bytes 8192

commit v2 on v1

--- a/solution.py
+++ b/solution.py
@@ -14,6 +14,7 @@
 BF16 = jnp.bfloat16
 LANES = 128
 K_CHUNK = 1280
+CHUNKS = 2
 
 
 def split2(v):
@@ -29,6 +30,7 @@
 def kernel(
     n_row,
     n_col,
+    n_x,
     gx,
     rx,
     w,
@@ -75,6 +77,8 @@
     rq = rows // LANES
     cq = cols // LANES
     total = n_row * n_col * per
+    n_y = n_col // n_x
+    n_a = n_b = n_x
     kappa = 1.0 / (EPSILON * math.log(2.0))
     log2w = -math.log2(total)
 
@@ -105,11 +109,30 @@
     loads[2].start()
     loads[3].start()
 
+    core = lax.rem(my_r, 2)
+    px = my_c // n_y
+    py = lax.rem(my_c, n_y)
+
+    def z_index(d):
+        return lax.rem(my_r + 2 * d + 2 * n_row, n_row)
+
+    def partner_of(r):
+        return r + 1 - 2 * core
+
+    def ab_index(da, db):
+        dx = da + (db - da) * core
+        dy = db + (da - db) * core
+        return lax.rem(px + dx + 2 * n_x, n_x) * n_y + lax.rem(py + dy + 2 * n_y, n_y)
+
+    n_z = n_row // 2
+    zdev = {d % n_z: (z_index(d), my_c) for d in (1, -1, 2, -2) if d % n_z}
+    adev = {d % n_a: (my_r, ab_index(d, 0)) for d in (1, -1, 2) if d % n_a}
+    bdev = {d % n_b: (my_r, ab_index(0, d)) for d in (1, -1, 2) if d % n_b}
+    pdev = (partner_of(my_r), my_c)
+    near = [*zdev.values(), *adev.values(), *bdev.values(), pdev]
     barrier = pltpu.get_barrier_semaphore()
-    for d in range(1, n_row):
-        pl.semaphore_signal(barrier, inc=1, device_id=row_peer(d), device_id_type=MESH)
-    for d in range(1, n_col):
-        pl.semaphore_signal(barrier, inc=1, device_id=col_peer(d), device_id_type=MESH)
+    for dev in near:
+        pl.semaphore_signal(barrier, inc=1, device_id=dev, device_id_type=MESH)
 
     loads[0].wait()
     loads[1].wait()
@@ -130,30 +153,94 @@
     gf[my_c] = feats[:per]
     rf[my_r] = feats[per:]
 
-    pl.semaphore_wait(barrier, n_row + n_col - 2)
-
-    gather = []
-    for d in range(1, n_row):
-        gather.append(
-            pltpu.make_async_remote_copy(
-                rf.at[my_r], rf.at[my_r], gsend.at[0], grecv.at[0], device_id=row_peer(d), device_id_type=MESH
-            )
-        )
-    for d in range(1, n_col):
-        gather.append(
-            pltpu.make_async_remote_copy(
-                gf.at[my_c], gf.at[my_c], gsend.at[1], grecv.at[1], device_id=col_peer(d), device_id_type=MESH
-            )
-        )
-    for cp in gather:
-        cp.start()
+    pl.semaphore_wait(barrier, len(near))
+
+    ch = per // CHUNKS
+
+    def piece(ref, block, c):
+        return ref.at[block, pl.ds(c * ch, ch)]
+
+    def send(ref, block, c, dev, slot, which):
+        pltpu.make_async_remote_copy(
+            piece(ref, block, c),
+            piece(ref, block, c),
+            gsend.at[which],
+            grecv.at[slot],
+            device_id=dev,
+            device_id_type=MESH,
+        ).start()
+
+    def arrived(ref, block, c, slot):
+        v = piece(ref, block, c)
+        pltpu.make_async_copy(v, v, grecv.at[slot]).wait()
+
+    halves = {1: range(CHUNKS // 2), -1: range(CHUNKS // 2, CHUNKS)}
+
+    def reach(n, c):
+        out = []
+        for s in (1, -1):
+            far = n // 2 if c in halves[s] else (n - 1) // 2
+            out += [(s, h) for h in range(1, far + 1)]
+        return out
+
+    order = []
+    for c in range(CHUNKS):
+        for s, h in reach(n_z, c):
+            order.append((h if h <= 2 else h + 3, 1 if h <= 2 else 2, c, "z", s * h, 0))
+        for sb, hb in reach(n_b, c):
+            order.append((hb + 2, 1, c, "b", 0, sb * hb))
+        for sa, ha in reach(n_a, c):
+            order.append((ha, 1, c, "a", sa * ha, 0))
+            for sb, hb in reach(n_b, c):
+                order.append((ha + hb + 3, 2, c, "b", sa * ha, sb * hb))
+    order.sort(key=lambda o: (o[0], o[2]))
+    slots = {o[2:]: n for n, o in enumerate(order)}
+    last = len(slots)
+
+    def to_z(c, block, d, step):
+        send(rf, block, c, zdev[step % n_z], slots[(c, "z", d, 0)], 0)
+
+    def to_partner(block, c):
+        send(rf, block, c, pdev, last, 0)
+
+    def to_a(c, d):
+        send(gf, my_c, c, adev[d % n_a], slots[(c, "a", d, 0)], 1)
+
+    def to_b(c, a):
+        for s, h in reach(n_b, c):
+            send(gf, ab_index(-a, 0), c, bdev[s * h % n_b], slots[(c, "b", a, s * h)], 1)
+
+    for c in range(CHUNKS):
+        for s, h in sorted(reach(n_z, c), key=lambda o: -o[1]):
+            if h <= 2:
+                to_z(c, my_r, s * h, s * h)
+        for s, h in reach(n_a, c):
+            to_a(c, s * h)
+    for c in range(CHUNKS):
+        to_b(c, 0)
+        to_partner(my_r, c)
+    for _, _, c, kind, p, q in order:
+        slot = slots[(c, kind, p, q)]
+        if kind == "z":
+            block = z_index(-p)
+            arrived(rf, block, c, slot)
+            s = 1 if p > 0 else -1
+            if p * s == 2:
+                for h in (4, 3):
+                    if (s, h) in reach(n_z, c):
+                        to_z(c, block, s * h, s * (h - 2))
+            to_partner(block, c)
+        elif p and not q:
+            arrived(gf, ab_index(-p, 0), c, slot)
+            to_b(c, p)
+        else:
+            arrived(gf, ab_index(-p, -q), c, slot)
 
     def all_bytes(ref, count, sem):
         view = ref.at[pl.ds(0, count)]
         return pltpu.make_async_copy(view, view, sem)
 
-    all_bytes(rf, n_row - 1, grecv.at[0]).wait()
-    all_bytes(gf, n_col - 1, grecv.at[1]).wait()
+    all_bytes(rf, n_z, grecv.at[last]).wait()
 
     scale = 2.0 * kappa / feat
     half = cq
@@ -229,7 +316,7 @@
         all_bytes(dst, count - 1, erecv.at[n]).wait()
         return cps
 
-    sent = list(gather)
+    sent = []
 
     phi0 = -kappa * sqr[...] + log2w
     ph = wide(phi0, RB)
@@ -361,7 +448,7 @@
     dma = pltpu.SemaphoreType.DMA
     n_chunks = max(1, vox // K_CHUNK + 1)
     g8, f2 = pl.pallas_call(
-        functools.partial(kernel, n_row, n_col),
+        functools.partial(kernel, n_row, n_col, math.isqrt(n_col)),
         out_shape=(jax.ShapeDtypeStruct((rq, LANES), F32), jax.ShapeDtypeStruct((n_row, per), F32)),
         in_specs=[hbm] * 5,
         out_specs=(vmem, vmem),
@@ -391,7 +478,7 @@
             dma((n_chunks,)),
             dma((2,)),
             dma((2,)),
-            dma((2,)),
+            dma((CHUNKS * (n_row // 2 + n_col),)),
             dma((6,)),
             dma((6,)),
         ],

time: 83.3 us -> 72.2 us (0.87)
  Pallas kernels: 79.9 us -> 68.8 us
    pallas_call x1, Pallas kernels: 79.9 us -> 68.8 us  [body(): pl.pallas_call(functools.partial(kernel, n_row, n_col, math.isqrt(n_col))...]
where the time goes in v2:
time: 72.2 us; the launch traced here: 72 us
  Pallas kernels  68.8 us (95%)
  local copies, waits for them, and re-layouts  2.56 us (4%)
    pallas_call x1, Pallas kernels, body(): pl.pallas_call(functools.partial(kernel, n_row, n_col, math.isqrt(n_col))...  68.8 us
    unnamed x2, local copies, waits for them, and re-layouts  2.56 us

profile of v2, /device:TPU:1, one launch (start us, length us, event | category | flops | bytes accessed | tf_op | source)
XLA Modules:
  0.0 72.0 jit_solution(5972466260785464700)
XLA Ops:
  0.6 68.8 %shard_map.68 = (f32[8,128]{1,0:T(8,128)}, f32[16,64]{1,0:T(8,128)}) custom-call(bf16[64,6480]{1,0:T(8,128)(2,1)} %gx.1, bf16[64,6480]{1,0:T(8,128)(2,1)} %rx.1, bf16[6480,512]{1,0:T(8,128)(2,1)} %w.1, f32[1,512]{1,0:T(1,128)} %bitcast.3, bf16[512,256]{1,0:T(8,128)(2,1)} %wo.1), custom_call_target="tpu_custom_call" | custom-call | tf_op jit(solution)/shard_map/pallas_call | solution.py:450
  69.4 1.3 %copy.9 = f32[1024]{0:T(1024)} copy(f32[1024]{0:T(1024)} %bitcast.2) | data formatting | bytes 8192
  70.7 1.3 %copy.10 = f32[16,64]{1,0:T(8,128)} copy(f32[16,64]{1,0:T(8,128)} %get-tuple-element.9) | data formatting | bytes 8192

commit v3 on v2

--- a/solution.py
+++ b/solution.py
@@ -13,7 +13,7 @@
 F32 = jnp.float32
 BF16 = jnp.bfloat16
 LANES = 128
-K_CHUNK = 1280
+K_CUTS = (1920, 3840, 5760)
 CHUNKS = 2
 
 
@@ -54,11 +54,10 @@
     colv,
     sqg,
     sqr,
-    send1,
-    recv1g,
-    recv1f,
-    send2,
-    recv2,
+    tops,
+    sums,
+    send_v,
+    recv,
     x_sem,
     w_sem,
     s_sem,
@@ -94,9 +93,7 @@
         pltpu.make_async_copy(b, b_v, s_sem.at[0]),
         pltpu.make_async_copy(wo, wo_v, s_sem.at[1]),
     ]
-    bounds = list(range(0, vox, K_CHUNK)) + [vox]
-    if bounds[-1] - bounds[-2] < K_CHUNK // 2 and len(bounds) > 2:
-        del bounds[-2]
+    bounds = sorted({0, vox, *(k for k in K_CUTS if k < vox)})
     spans = list(zip(bounds[:-1], bounds[1:]))
     wloads = [
         pltpu.make_async_copy(w.at[pl.ds(k0, k1 - k0)], w_v.at[pl.ds(k0, k1 - k0)], w_sem.at[n])
@@ -283,10 +280,10 @@
     def lane_groups(v):
         return [v[:, q * LANES : (q + 1) * LANES] for q in range(cq)]
 
-    def to_dense(src, dst, row0, op):
+    def to_dense(src, dst, op):
         for q in range(rq):
             blk = src[pl.ds(q * LANES, LANES), :].T
-            dst[pl.ds(row0 + q, 1), :] = op(blk, axis=0, keepdims=True)
+            dst[pl.ds(q, 1), :] = op(blk, axis=0, keepdims=True)
 
     def to_col(x8):
         for q in range(rq):
@@ -303,85 +300,73 @@
 
     add = lambda p, q: p + q
 
-    def exchange(n, src, dst, me, peer, count):
-        dst[me] = src[...]
-        cps = [
+    def exchange(n, me, peer, count):
+        recv[n, me] = send_v[n]
+        for d in range(1, count):
             pltpu.make_async_remote_copy(
-                src, dst.at[me], esend.at[n], erecv.at[n], device_id=peer(d), device_id_type=MESH
-            )
-            for d in range(1, count)
-        ]
-        for cp in cps:
-            cp.start()
-        all_bytes(dst, count - 1, erecv.at[n]).wait()
-        return cps
-
-    sent = []
-
-    phi0 = -kappa * sqr[...] + log2w
-    ph = wide(phi0, RB)
-
-    def gen_max(off):
-        t = lane_groups(tile[pl.ds(off, RB), :])
-        m = tree(jnp.maximum, [a + p for a, p in zip(t, ph)])
-        part[pl.ds(off, RB), :] = jnp.broadcast_to(jnp.max(m, axis=1, keepdims=True), (RB, LANES))
-
-    blocks(gen_max)
-
-    def gen_sum(off):
-        m = part[pl.ds(off, RB), :]
-        t = lane_groups(tile[pl.ds(off, RB), :])
-        part2[pl.ds(off, RB), :] = tree(add, [jnp.exp2((a + p) - m) for a, p in zip(t, ph)])
-
-    blocks(gen_sum)
-    to_dense(part, send1, 0, jnp.max)
-    to_dense(part2, send1, rq, jnp.sum)
-    sent += exchange(0, send1, recv1g, my_c, col_peer, n_col)
-
-    def lse2(ref, count, q):
-        ms = [ref[k, 0:q, :] for k in range(count)]
-        m = tree(jnp.maximum, ms)
-        s = tree(add, [ref[k, q:, :] * jnp.exp2(ms[k] - m) for k in range(count)])
-        return m + jnp.log2(s)
-
-    gamma = -lse2(recv1g, n_col, rq)
+                send_v.at[n], recv.at[n, me], esend.at[n], erecv.at[n], device_id=peer(d), device_id_type=MESH
+            ).start()
+        all_bytes(recv.at[n], count - 1, erecv.at[n]).wait()
+        return [recv[n, k] for k in range(count)]
+
+    def lse2(ls):
+        m = tree(jnp.maximum, ls)
+        return m + jnp.log2(tree(add, [jnp.exp2(v - m) for v in ls]))
+
+    ph = wide(-kappa * sqr[...] + log2w, RB)
+
+    def gen_first(off):
+        t = [a + p for a, p in zip(lane_groups(tile[pl.ds(off, RB), :]), ph)]
+        m = tree(jnp.maximum, t)
+        part[pl.ds(off, RB), :] = m
+        part2[pl.ds(off, RB), :] = tree(add, [jnp.exp2(v - m) for v in t])
+
+    blocks(gen_first)
+    for q in range(rq):
+        m = part[pl.ds(q * LANES, LANES), :].T
+        s = part2[pl.ds(q * LANES, LANES), :].T
+        top = jnp.max(m, axis=0, keepdims=True)
+        tops[pl.ds(q, 1), :] = top
+        sums[pl.ds(q, 1), :] = jnp.sum(s * jnp.exp2(m - top), axis=0, keepdims=True)
+    send_v[0] = tops[...] + jnp.log2(sums[...])
+    gamma = -lse2(exchange(0, my_c, col_peer, n_col))
     to_col(gamma + log2w)
 
+    def col_slab(off, q):
+        return tile.at[pl.ds(off, RB), pl.ds(q * LANES, LANES)]
+
+    def fold(op, v):
+        return tree(op, [v[8 * k : 8 * k + 8] for k in range(RB // 8)])
+
     def ref_max(n, ms):
+        off = pl.multiple_of(n * RB, RB)
+        c = colv[pl.ds(off, RB), :]
+        return tuple(jnp.maximum(ms[q], fold(jnp.maximum, col_slab(off, q)[...] + c)) for q in range(cq))
+
+    low = jnp.full((8, LANES), -jnp.inf, F32)
+    ms = lax.fori_loop(0, rows // RB, ref_max, tuple(low for _ in range(cq)))
+    for q in range(cq):
+        tops[pl.ds(q, 1), :] = jnp.max(ms[q], axis=0, keepdims=True)
+    cm = tops[...]
+    cmb = wide(cm, RB)
+
+    def ref_sum(n, ss):
         off = pl.multiple_of(n * RB, RB)
         c = colv[pl.ds(off, RB), :]
         out = []
         for q in range(cq):
-            t = tile[pl.ds(off, RB), q * LANES : (q + 1) * LANES] + c
-            tile[pl.ds(off, RB), q * LANES : (q + 1) * LANES] = t
-            out.append(jnp.maximum(ms[q], tree(jnp.maximum, [t[8 * k : 8 * k + 8] for k in range(RB // 8)])))
-        return tuple(out)
-
-    low = jnp.full((8, LANES), -jnp.inf, F32)
-    ms = lax.fori_loop(0, rows // RB, ref_max, tuple(low for _ in range(cq)))
-    cm = [jnp.max(m, axis=0, keepdims=True) for m in ms]
-    cmb = [jnp.broadcast_to(m, (RB, LANES)) for m in cm]
-
-    def fold(v):
-        return tree(add, [v[8 * k : 8 * k + 8] for k in range(RB // 8)])
-
-    def ref_sum(n, ss):
-        off = pl.multiple_of(n * RB, RB)
-        out = []
-        for q in range(cq):
-            e = jnp.exp2(tile[pl.ds(off, RB), q * LANES : (q + 1) * LANES] - cmb[q])
-            tile[pl.ds(off, RB), q * LANES : (q + 1) * LANES] = e
-            out.append(ss[q] + fold(e))
+            e = jnp.exp2(col_slab(off, q)[...] + (c - cmb[q]))
+            col_slab(off, q)[...] = e
+            out.append(ss[q] + fold(add, e))
         return tuple(out)
 
     zero = jnp.zeros((8, LANES), F32)
     ss = lax.fori_loop(0, rows // RB, ref_sum, tuple(zero for _ in range(cq)))
     for q in range(cq):
-        send2[pl.ds(q, 1), :] = cm[q]
-        send2[pl.ds(cq + q, 1), :] = jnp.sum(ss[q], axis=0, keepdims=True)
-    sent += exchange(1, send2, recv1f, my_r, row_peer, n_row)
-    phi = -lse2(recv1f, n_row, cq)
-    w8 = jnp.exp2(send2[0:cq, :] + phi)
+        sums[pl.ds(q, 1), :] = jnp.sum(ss[q], axis=0, keepdims=True)
+    send_v[1] = cm + jnp.log2(sums[...])
+    phi = -lse2(exchange(1, my_r, row_peer, n_row))
+    w8 = jnp.exp2(cm + phi)
 
     def gen_pass(n, scale8):
         vw = wide(scale8, RB)
@@ -391,10 +376,8 @@
             part[pl.ds(off, RB), :] = tree(add, [a * p for a, p in zip(t, vw)])
 
         blocks(body)
-        src = send1.at[pl.ds(0, rq)] if n == 2 else send1.at[pl.ds(rq, rq)]
-        to_dense(part, send1, 0 if n == 2 else rq, jnp.sum)
-        cps = exchange(n, src, recv2.at[n - 2], my_c, col_peer, n_col)
-        return tree(add, [recv2[n - 2, k] for k in range(n_col)]), cps
+        to_dense(part, send_v.at[n], jnp.sum)
+        return tree(add, exchange(n, my_c, col_peer, n_col))
 
     def ref_pass(n, scale8):
         to_col(scale8)
@@ -402,25 +385,17 @@
         def step(k, ss):
             off = pl.multiple_of(k * RB, RB)
             c = colv[pl.ds(off, RB), :]
-            return tuple(
-                ss[q] + fold(tile[pl.ds(off, RB), q * LANES : (q + 1) * LANES] * c) for q in range(cq)
-            )
+            return tuple(ss[q] + fold(add, col_slab(off, q)[...] * c) for q in range(cq))
 
         ss = lax.fori_loop(0, rows // RB, step, tuple(zero for _ in range(cq)))
-        row0 = 0 if n == 3 else cq
         for q in range(cq):
-            send2[pl.ds(row0 + q, 1), :] = w8[q : q + 1, :] * jnp.sum(ss[q], axis=0, keepdims=True)
-        cps = exchange(n, send2.at[pl.ds(row0, cq)], recv2.at[n - 2], my_r, row_peer, n_row)
-        return tree(add, [recv2[n - 2, k] for k in range(n_row)]), cps
-
-    def drain(n, ref, count):
-        all_bytes(ref, count, esend.at[n]).wait()
-
-    drain(0, recv1g, n_col - 1)
-    r, cps = gen_pass(2, w8)
-    drain(1, recv1f, n_row - 1)
-    c, cps = ref_pass(3, 1.0 / r)
-    r, cps = gen_pass(4, w8 / c)
+            sums[pl.ds(q, 1), :] = jnp.sum(ss[q], axis=0, keepdims=True)
+        send_v[n] = w8 * sums[...]
+        return tree(add, exchange(n, my_r, row_peer, n_row))
+
+    r = gen_pass(2, w8)
+    c = ref_pass(3, 1.0 / r)
+    r = gen_pass(4, w8 / c)
     for q in range(rq):
         per_q = LANES // per
         v = jnp.concatenate([gf[q * per_q + k] for k in range(per_q)], axis=0)
@@ -428,12 +403,12 @@
         s = functools.reduce(add, [v[:, k * LANES : (k + 1) * LANES] for k in range(feat // LANES)])
         sqg[pl.ds(q, 1), :] = jnp.sum(s.T, axis=0, keepdims=True) * (1.0 / feat)
     g_out[...] = (gamma - jnp.log2(r)) * (1.0 / kappa) + sqg[...]
-    c, cps = ref_pass(5, 1.0 / r)
+    c = ref_pass(5, 1.0 / r)
     f = (phi - jnp.log2(c)) * (1.0 / kappa) + sqr[...]
     f_out[pl.ds(0, half), :] = f[:, :per]
     f_out[pl.ds(half, half), :] = f[:, per:]
-    for n, count in ((2, n_col), (3, n_row), (4, n_col), (5, n_row)):
-        drain(n, recv2.at[n - 2], count - 1)
+    for n in range(6):
+        all_bytes(recv.at[n], (n_row if n % 2 else n_col) - 1, esend.at[n]).wait()
     all_bytes(rf, n_row - 1, gsend.at[0]).wait()
     all_bytes(gf, n_col - 1, gsend.at[1]).wait()
 
@@ -446,10 +421,10 @@
     hbm = pl.BlockSpec(memory_space=pl.ANY)
     vmem = pl.BlockSpec(memory_space=pltpu.VMEM)
     dma = pltpu.SemaphoreType.DMA
-    n_chunks = max(1, vox // K_CHUNK + 1)
+    n_chunks = len(K_CUTS) + 1
     g8, f2 = pl.pallas_call(
         functools.partial(kernel, n_row, n_col, math.isqrt(n_col)),
-        out_shape=(jax.ShapeDtypeStruct((rq, LANES), F32), jax.ShapeDtypeStruct((n_row, per), F32)),
+        out_shape=(pltpu.VMEM((rq, LANES), F32), pltpu.VMEM((n_row, per), F32)),
         in_specs=[hbm] * 5,
         out_specs=(vmem, vmem),
         scratch_shapes=[
@@ -469,11 +444,10 @@
             pltpu.VMEM((rows, LANES), F32),
             pltpu.VMEM((rq, LANES), F32),
             pltpu.VMEM((cq, LANES), F32),
-            pltpu.VMEM((2 * rq, LANES), F32),
-            pltpu.VMEM((n_col, 2 * rq, LANES), F32),
-            pltpu.VMEM((n_row, 2 * cq, LANES), F32),
-            pltpu.VMEM((2 * cq, LANES), F32),
-            pltpu.VMEM((4, max(n_col, n_row), max(rq, cq), LANES), F32),
+            pltpu.VMEM((rq, LANES), F32),
+            pltpu.VMEM((cq, LANES), F32),
+            pltpu.VMEM((6, rq, LANES), F32),
+            pltpu.VMEM((6, max(n_col, n_row), rq, LANES), F32),
             dma((2,)),
             dma((n_chunks,)),
             dma((2,)),

time: 72.2 us -> 66 us (0.914)
  Pallas kernels: 68.8 us -> 64.1 us
  local copies, waits for them, and re-layouts: 2.56 us -> 1.19 us
    pallas_call x1, Pallas kernels: 68.8 us -> 64.1 us  [body(): pl.pallas_call(functools.partial(kernel, n_row, n_col, math.isqrt(n_col))...]
    unnamed x2, local copies, waits for them, and re-layouts: 2.56 us -> 1.19 us
where the time goes in v3:
time: 66 us; the launch traced here: 65.9 us
  Pallas kernels  64.1 us (97%)
  local copies, waits for them, and re-layouts  1.19 us (2%)
    pallas_call x1, Pallas kernels, body(): pl.pallas_call(functools.partial(kernel, n_row, n_col, math.isqrt(n_col))...  64.1 us

profile of v3, /device:TPU:1, one launch (start us, length us, event | category | flops | bytes accessed | tf_op | source)
XLA Modules:
  0.0 65.9 jit_solution(12360300076987825757)
XLA Ops:
  0.6 64.1 %shard_map.68 = (f32[8,128]{1,0:T(8,128)S(1)}, f32[16,64]{1,0:T(8,128)S(1)}) custom-call(bf16[64,6480]{1,0:T(8,128)(2,1)} %gx.1, bf16[64,6480]{1,0:T(8,128)(2,1)} %rx.1, bf16[6480,512]{1,0:T(8,128)(2,1)} %w.1, f32[1,512]{1,0:T(1,128)} %bitcast.3, bf16[512,256]{1,0:T(8,128)(2,1)} %wo.1), custom_call_target="tpu_custom_call" | custom-call | tf_op jit(solution)/shard_map/pallas_call | solution.py:425
  64.7 0.6 copy.9
  65.3 0.6 copy.10

commit v4 on v3

--- a/solution.py
+++ b/solution.py
@@ -13,7 +13,7 @@
 F32 = jnp.float32
 BF16 = jnp.bfloat16
 LANES = 128
-K_CUTS = (1920, 3840, 5760)
+K_CUTS = (2176, 4352)
 CHUNKS = 2
 
 
@@ -81,12 +81,6 @@
     kappa = 1.0 / (EPSILON * math.log(2.0))
     log2w = -math.log2(total)
 
-    def row_peer(d):
-        return (lax.rem(my_r + d, n_row), my_c)
-
-    def col_peer(d):
-        return (my_r, lax.rem(my_c + d, n_col))
-
     loads = [
         pltpu.make_async_copy(gx, x_v.at[pl.ds(0, per)], x_sem.at[0]),
         pltpu.make_async_copy(rx, x_v.at[pl.ds(per, per)], x_sem.at[1]),
@@ -178,19 +172,19 @@
         for s in (1, -1):
             far = n // 2 if c in halves[s] else (n - 1) // 2
             out += [(s, h) for h in range(1, far + 1)]
-        return out
+        return sorted(out, key=lambda o: -o[1])
 
     order = []
     for c in range(CHUNKS):
         for s, h in reach(n_z, c):
-            order.append((h if h <= 2 else h + 3, 1 if h <= 2 else 2, c, "z", s * h, 0))
+            order.append(({1: 1, 2: 0}.get(h, 2), c, c, "z", s * h, 0))
         for sb, hb in reach(n_b, c):
-            order.append((hb + 2, 1, c, "b", 0, sb * hb))
+            order.append((3, c, c, "b", 0, sb * hb))
         for sa, ha in reach(n_a, c):
-            order.append((ha, 1, c, "a", sa * ha, 0))
+            order.append((0, c, c, "a", sa * ha, 0))
             for sb, hb in reach(n_b, c):
-                order.append((ha + hb + 3, 2, c, "b", sa * ha, sb * hb))
-    order.sort(key=lambda o: (o[0], o[2]))
+                order.append((4, c, c, "b", sa * ha, sb * hb))
+    order.sort(key=lambda o: o[:2])
     slots = {o[2:]: n for n, o in enumerate(order)}
     last = len(slots)
 
@@ -208,13 +202,17 @@
             send(gf, ab_index(-a, 0), c, bdev[s * h % n_b], slots[(c, "b", a, s * h)], 1)
 
     for c in range(CHUNKS):
-        for s, h in sorted(reach(n_z, c), key=lambda o: -o[1]):
-            if h <= 2:
+        for s, h in reach(n_z, c):
+            if h == 2:
                 to_z(c, my_r, s * h, s * h)
         for s, h in reach(n_a, c):
             to_a(c, s * h)
     for c in range(CHUNKS):
+        for s, h in reach(n_z, c):
+            if h == 1:
+                to_z(c, my_r, s * h, s * h)
         to_b(c, 0)
+    for c in range(CHUNKS):
         to_partner(my_r, c)
     for _, _, c, kind, p, q in order:
         slot = slots[(c, kind, p, q)]
@@ -300,14 +298,25 @@
 
     add = lambda p, q: p + q
 
-    def exchange(n, me, peer, count):
+    def ring(n, d):
+        return min(d, n - d)
+
+    zk = [(d, k) for d in range(n_z) for k in range(2) if d or k]
+    zk.sort(key=lambda o: -ring(n_z, o[0]))
+    zrow = {d: z_index(d) for d in range(n_z)}
+    row_peers = [(partner_of(zrow[d]) if k else zrow[d], my_c) for d, k in zk]
+    xy = [(i, j) for i in range(n_a) for j in range(n_b) if i or j]
+    xy.sort(key=lambda o: -ring(n_a, o[0]) - ring(n_b, o[1]))
+    col_peers = [(my_r, ab_index(*o)) for o in xy]
+
+    def exchange(n, me, peers):
+        for dev in peers:
+            pltpu.make_async_remote_copy(
+                send_v.at[n], recv.at[n, me], esend.at[n], erecv.at[n], device_id=dev, device_id_type=MESH
+            ).start()
         recv[n, me] = send_v[n]
-        for d in range(1, count):
-            pltpu.make_async_remote_copy(
-                send_v.at[n], recv.at[n, me], esend.at[n], erecv.at[n], device_id=peer(d), device_id_type=MESH
-            ).start()
-        all_bytes(recv.at[n], count - 1, erecv.at[n]).wait()
-        return [recv[n, k] for k in range(count)]
+        all_bytes(recv.at[n], len(peers), erecv.at[n]).wait()
+        return [recv[n, k] for k in range(len(peers) + 1)]
 
     def lse2(ls):
         m = tree(jnp.maximum, ls)
@@ -329,7 +338,7 @@
         tops[pl.ds(q, 1), :] = top
         sums[pl.ds(q, 1), :] = jnp.sum(s * jnp.exp2(m - top), axis=0, keepdims=True)
     send_v[0] = tops[...] + jnp.log2(sums[...])
-    gamma = -lse2(exchange(0, my_c, col_peer, n_col))
+    gamma = -lse2(exchange(0, my_c, col_peers))
     to_col(gamma + log2w)
 
     def col_slab(off, q):
@@ -365,7 +374,7 @@
     for q in range(cq):
         sums[pl.ds(q, 1), :] = jnp.sum(ss[q], axis=0, keepdims=True)
     send_v[1] = cm + jnp.log2(sums[...])
-    phi = -lse2(exchange(1, my_r, row_peer, n_row))
+    phi = -lse2(exchange(1, my_r, row_peers))
     w8 = jnp.exp2(cm + phi)
 
     def gen_pass(n, scale8):
@@ -377,7 +386,7 @@
 
         blocks(body)
         to_dense(part, send_v.at[n], jnp.sum)
-        return tree(add, exchange(n, my_c, col_peer, n_col))
+        return tree(add, exchange(n, my_c, col_peers))
 
     def ref_pass(n, scale8):
         to_col(scale8)
@@ -391,7 +400,7 @@
         for q in range(cq):
             sums[pl.ds(q, 1), :] = jnp.sum(ss[q], axis=0, keepdims=True)
         send_v[n] = w8 * sums[...]
-        return tree(add, exchange(n, my_r, row_peer, n_row))
+        return tree(add, exchange(n, my_r, row_peers))
 
     r = gen_pass(2, w8)
     c = ref_pass(3, 1.0 / r)

time: 66 us -> 63.4 us (0.961)
  Pallas kernels: 64.1 us -> 61.5 us
    pallas_call x1, Pallas kernels: 64.1 us -> 61.5 us  [body(): pl.pallas_call(functools.partial(kernel, n_row, n_col, math.isqrt(n_col))...]
where the time goes in v4:
time: 63.4 us; the launch traced here: 63.3 us
  Pallas kernels  61.5 us (97%)
  local copies, waits for them, and re-layouts  1.19 us (2%)
  between operations  0.64 us (1%)
    pallas_call x1, Pallas kernels, body(): pl.pallas_call(functools.partial(kernel, n_row, n_col, math.isqrt(n_col))...  61.5 us

profile of v4, /device:TPU:1, one launch (start us, length us, event | category | flops | bytes accessed | tf_op | source)
XLA Modules:
  0.0 63.3 jit_solution(12463073443131748026)
XLA Ops:
  0.6 61.5 %shard_map.68 = (f32[8,128]{1,0:T(8,128)S(1)}, f32[16,64]{1,0:T(8,128)S(1)}) custom-call(bf16[64,6480]{1,0:T(8,128)(2,1)} %gx.1, bf16[64,6480]{1,0:T(8,128)(2,1)} %rx.1, bf16[6480,512]{1,0:T(8,128)(2,1)} %w.1, f32[1,512]{1,0:T(1,128)} %bitcast.3, bf16[512,256]{1,0:T(8,128)(2,1)} %wo.1), custom_call_target="tpu_custom_call" | custom-call | tf_op jit(solution)/shard_map/pallas_call | solution.py:434
  62.1 0.6 copy.9
  62.7 0.6 copy.10

commit v5 on v4

--- a/solution.py
+++ b/solution.py
@@ -15,6 +15,8 @@
 LANES = 128
 K_CUTS = (2176, 4352)
 CHUNKS = 2
+RB = 32
+UNROLL = 4
 
 
 def split2(v):
@@ -214,38 +216,34 @@
         to_b(c, 0)
     for c in range(CHUNKS):
         to_partner(my_r, c)
-    for _, _, c, kind, p, q in order:
-        slot = slots[(c, kind, p, q)]
-        if kind == "z":
-            block = z_index(-p)
-            arrived(rf, block, c, slot)
-            s = 1 if p > 0 else -1
-            if p * s == 2:
-                for h in (4, 3):
-                    if (s, h) in reach(n_z, c):
-                        to_z(c, block, s * h, s * (h - 2))
-            to_partner(block, c)
-        elif p and not q:
-            arrived(gf, ab_index(-p, 0), c, slot)
-            to_b(c, p)
-        else:
-            arrived(gf, ab_index(-p, -q), c, slot)
-
     def all_bytes(ref, count, sem):
         view = ref.at[pl.ds(0, count)]
         return pltpu.make_async_copy(view, view, sem)
 
-    all_bytes(rf, n_z, grecv.at[last]).wait()
+    def take(some):
+        for level, _, c, kind, p, q in order:
+            if level not in some:
+                continue
+            slot = slots[(c, kind, p, q)]
+            if kind == "z":
+                block = z_index(-p)
+                arrived(rf, block, c, slot)
+                s = 1 if p > 0 else -1
+                if p * s == 2:
+                    for h in (4, 3):
+                        if (s, h) in reach(n_z, c):
+                            to_z(c, block, s * h, s * (h - 2))
+                to_partner(block, c)
+            elif p and not q:
+                arrived(gf, ab_index(-p, 0), c, slot)
+                to_b(c, p)
+            else:
+                arrived(gf, ab_index(-p, -q), c, slot)
 
     scale = 2.0 * kappa / feat
     half = cq
-
-    for q in range(rq):
-        per_q = LANES // per
-        v = jnp.concatenate([gf[q * per_q + k] for k in range(per_q)], axis=0)
-        hi, lo = split2(v * scale)
-        g_hi[pl.ds(q * LANES, LANES), :] = hi
-        g_lo[pl.ds(q * LANES, LANES), :] = lo
+    take((0, 1, 2, 3))
+    all_bytes(rf, n_z, grecv.at[last]).wait()
     for q in range(cq):
         v = jnp.concatenate([rf[q], rf[q + half]], axis=0)
         vt = v.T
@@ -253,8 +251,15 @@
         hi, lo = split2(vt)
         r_hi[:, pl.ds(q * LANES, LANES)] = hi
         r_lo[:, pl.ds(q * LANES, LANES)] = lo
-
-    nt = 256
+    take((4,))
+    for q in range(rq):
+        per_q = LANES // per
+        v = jnp.concatenate([gf[q * per_q + k] for k in range(per_q)], axis=0)
+        hi, lo = split2(v * scale)
+        g_hi[pl.ds(q * LANES, LANES), :] = hi
+        g_lo[pl.ds(q * LANES, LANES), :] = lo
+
+    nt = min(1024, cols)
 
     def tile_step(n, _):
         off = pl.multiple_of(n * nt, nt)
@@ -266,14 +271,12 @@
 
     lax.fori_loop(0, cols // nt, tile_step, 0)
 
-    RB = 32
-
     def blocks(body):
         def step(n, _):
             body(pl.multiple_of(n * RB, RB))
             return 0
 
-        lax.fori_loop(0, rows // RB, step, 0)
+        lax.fori_loop(0, rows // RB, step, 0, unroll=UNROLL)
 
     def lane_groups(v):
         return [v[:, q * LANES : (q + 1) * LANES] for q in range(cq)]
@@ -353,7 +356,7 @@
         return tuple(jnp.maximum(ms[q], fold(jnp.maximum, col_slab(off, q)[...] + c)) for q in range(cq))
 
     low = jnp.full((8, LANES), -jnp.inf, F32)
-    ms = lax.fori_loop(0, rows // RB, ref_max, tuple(low for _ in range(cq)))
+    ms = lax.fori_loop(0, rows // RB, ref_max, tuple(low for _ in range(cq)), unroll=UNROLL)
     for q in range(cq):
         tops[pl.ds(q, 1), :] = jnp.max(ms[q], axis=0, keepdims=True)
     cm = tops[...]
@@ -370,7 +373,7 @@
         return tuple(out)
 
     zero = jnp.zeros((8, LANES), F32)
-    ss = lax.fori_loop(0, rows // RB, ref_sum, tuple(zero for _ in range(cq)))
+    ss = lax.fori_loop(0, rows // RB, ref_sum, tuple(zero for _ in range(cq)), unroll=UNROLL)
     for q in range(cq):
         sums[pl.ds(q, 1), :] = jnp.sum(ss[q], axis=0, keepdims=True)
     send_v[1] = cm + jnp.log2(sums[...])
@@ -396,7 +399,7 @@
             c = colv[pl.ds(off, RB), :]
             return tuple(ss[q] + fold(add, col_slab(off, q)[...] * c) for q in range(cq))
 
-        ss = lax.fori_loop(0, rows // RB, step, tuple(zero for _ in range(cq)))
+        ss = lax.fori_loop(0, rows // RB, step, tuple(zero for _ in range(cq)), unroll=UNROLL)
         for q in range(cq):
             sums[pl.ds(q, 1), :] = jnp.sum(ss[q], axis=0, keepdims=True)
         send_v[n] = w8 * sums[...]

time: 63.4 us -> 61 us (0.962)
  Pallas kernels: 61.5 us -> 59.1 us
    pallas_call x1, Pallas kernels: 61.5 us -> 59.1 us  [body(): pl.pallas_call(functools.partial(kernel, n_row, n_col, math.isqrt(n_col))...]
where the time goes in v5:
time: 61 us; the launch traced here: 60.9 us
  Pallas kernels  59.1 us (97%)
  local copies, waits for them, and re-layouts  1.19 us (2%)
  between operations  0.64 us (1%)
    pallas_call x1, Pallas kernels, body(): pl.pallas_call(functools.partial(kernel, n_row, n_col, math.isqrt(n_col))...  59.1 us

profile of v5, /device:TPU:1, one launch (start us, length us, event | category | flops | bytes accessed | tf_op | source)
XLA Modules:
  0.0 60.9 jit_solution(6652169705288796866)
XLA Ops:
  0.6 59.1 %shard_map.68 = (f32[8,128]{1,0:T(8,128)S(1)}, f32[16,64]{1,0:T(8,128)S(1)}) custom-call(bf16[64,6480]{1,0:T(8,128)(2,1)} %gx.1, bf16[64,6480]{1,0:T(8,128)(2,1)} %rx.1, bf16[6480,512]{1,0:T(8,128)(2,1)} %w.1, f32[1,512]{1,0:T(1,128)} %bitcast.3, bf16[512,256]{1,0:T(8,128)(2,1)} %wo.1), custom_call_target="tpu_custom_call" | custom-call | tf_op jit(solution)/shard_map/pallas_call | solution.py:437
  59.7 0.6 copy.9
  60.3 0.6 copy.10

commit v6 on v5

--- a/solution.py
+++ b/solution.py
@@ -16,7 +16,7 @@
 K_CUTS = (2176, 4352)
 CHUNKS = 2
 RB = 32
-UNROLL = 4
+UNROLL = 8
 
 
 def split2(v):
@@ -46,10 +46,8 @@
     wo_v,
     gf,
     rf,
-    g_hi,
-    g_lo,
-    r_hi,
-    r_lo,
+    g_cat,
+    r_cat,
     tile,
     part,
     part2,
@@ -183,7 +181,7 @@
         for sb, hb in reach(n_b, c):
             order.append((3, c, c, "b", 0, sb * hb))
         for sa, ha in reach(n_a, c):
-            order.append((0, c, c, "a", sa * ha, 0))
+            order.append((0, c - (ha == 1) * 0.5, c, "a", sa * ha, 0))
             for sb, hb in reach(n_b, c):
                 order.append((4, c, c, "b", sa * ha, sb * hb))
     order.sort(key=lambda o: o[:2])
@@ -204,11 +202,11 @@
             send(gf, ab_index(-a, 0), c, bdev[s * h % n_b], slots[(c, "b", a, s * h)], 1)
 
     for c in range(CHUNKS):
+        for s, h in reach(n_a, c):
+            to_a(c, s * h)
         for s, h in reach(n_z, c):
             if h == 2:
                 to_z(c, my_r, s * h, s * h)
-        for s, h in reach(n_a, c):
-            to_a(c, s * h)
     for c in range(CHUNKS):
         for s, h in reach(n_z, c):
             if h == 1:
@@ -249,27 +247,17 @@
         vt = v.T
         sqr[pl.ds(q, 1), :] = jnp.sum(vt * vt, axis=0, keepdims=True) * (1.0 / feat)
         hi, lo = split2(vt)
-        r_hi[:, pl.ds(q * LANES, LANES)] = hi
-        r_lo[:, pl.ds(q * LANES, LANES)] = lo
+        for k, v in enumerate((hi, hi, lo)):
+            r_cat[pl.ds(k * feat, feat), q * LANES : (q + 1) * LANES] = v
     take((4,))
     for q in range(rq):
         per_q = LANES // per
         v = jnp.concatenate([gf[q * per_q + k] for k in range(per_q)], axis=0)
         hi, lo = split2(v * scale)
-        g_hi[pl.ds(q * LANES, LANES), :] = hi
-        g_lo[pl.ds(q * LANES, LANES), :] = lo
-
-    nt = min(1024, cols)
-
-    def tile_step(n, _):
-        off = pl.multiple_of(n * nt, nt)
-        rh = r_hi[:, pl.ds(off, nt)]
-        rl = r_lo[:, pl.ds(off, nt)]
-        gh = g_hi[...]
-        tile[:, pl.ds(off, nt)] = mm(gh, rh) + (mm(g_lo[...], rh) + mm(gh, rl))
-        return 0
-
-    lax.fori_loop(0, cols // nt, tile_step, 0)
+        for k, v in enumerate((hi, lo, hi)):
+            g_cat[pl.ds(q * LANES, LANES), k * feat : (k + 1) * feat] = v
+
+    tile[...] = mm(g_cat[...], r_cat[...])
 
     def blocks(body):
         def step(n, _):
@@ -312,18 +300,28 @@
     xy.sort(key=lambda o: -ring(n_a, o[0]) - ring(n_b, o[1]))
     col_peers = [(my_r, ab_index(*o)) for o in xy]
 
-    def exchange(n, me, peers):
+    def exchange(n, me, peers, meanwhile=None):
         for dev in peers:
             pltpu.make_async_remote_copy(
                 send_v.at[n], recv.at[n, me], esend.at[n], erecv.at[n], device_id=dev, device_id_type=MESH
             ).start()
         recv[n, me] = send_v[n]
+        if meanwhile is not None:
+            meanwhile()
         all_bytes(recv.at[n], len(peers), erecv.at[n]).wait()
         return [recv[n, k] for k in range(len(peers) + 1)]
 
     def lse2(ls):
         m = tree(jnp.maximum, ls)
         return m + jnp.log2(tree(add, [jnp.exp2(v - m) for v in ls]))
+
+    def gen_squares():
+        for q in range(rq):
+            per_q = LANES // per
+            v = jnp.concatenate([gf[q * per_q + k] for k in range(per_q)], axis=0)
+            v = v * v
+            s = functools.reduce(add, [v[:, k * LANES : (k + 1) * LANES] for k in range(feat // LANES)])
+            sqg[pl.ds(q, 1), :] = jnp.sum(s.T, axis=0, keepdims=True) * (1.0 / feat)
 
     ph = wide(-kappa * sqr[...] + log2w, RB)
 
@@ -341,7 +339,7 @@
         tops[pl.ds(q, 1), :] = top
         sums[pl.ds(q, 1), :] = jnp.sum(s * jnp.exp2(m - top), axis=0, keepdims=True)
     send_v[0] = tops[...] + jnp.log2(sums[...])
-    gamma = -lse2(exchange(0, my_c, col_peers))
+    gamma = -lse2(exchange(0, my_c, col_peers, gen_squares))
     to_col(gamma + log2w)
 
     def col_slab(off, q):
@@ -391,7 +389,7 @@
         to_dense(part, send_v.at[n], jnp.sum)
         return tree(add, exchange(n, my_c, col_peers))
 
-    def ref_pass(n, scale8):
+    def ref_pass(n, scale8, meanwhile=None):
         to_col(scale8)
 
         def step(k, ss):
@@ -403,26 +401,23 @@
         for q in range(cq):
             sums[pl.ds(q, 1), :] = jnp.sum(ss[q], axis=0, keepdims=True)
         send_v[n] = w8 * sums[...]
-        return tree(add, exchange(n, my_r, row_peers))
+        return tree(add, exchange(n, my_r, row_peers, meanwhile))
 
     r = gen_pass(2, w8)
     c = ref_pass(3, 1.0 / r)
     r = gen_pass(4, w8 / c)
-    for q in range(rq):
-        per_q = LANES // per
-        v = jnp.concatenate([gf[q * per_q + k] for k in range(per_q)], axis=0)
-        v = v * v
-        s = functools.reduce(add, [v[:, k * LANES : (k + 1) * LANES] for k in range(feat // LANES)])
-        sqg[pl.ds(q, 1), :] = jnp.sum(s.T, axis=0, keepdims=True) * (1.0 / feat)
-    g_out[...] = (gamma - jnp.log2(r)) * (1.0 / kappa) + sqg[...]
-    c = ref_pass(5, 1.0 / r)
+    def gen_result():
+        g_out[...] = (gamma - jnp.log2(r)) * (1.0 / kappa) + sqg[...]
+        for n in range(5):
+            all_bytes(recv.at[n], (n_row if n % 2 else n_col) - 1, esend.at[n]).wait()
+        all_bytes(rf, n_row - 1, gsend.at[0]).wait()
+        all_bytes(gf, n_col - 1, gsend.at[1]).wait()
+
+    c = ref_pass(5, 1.0 / r, gen_result)
     f = (phi - jnp.log2(c)) * (1.0 / kappa) + sqr[...]
     f_out[pl.ds(0, half), :] = f[:, :per]
     f_out[pl.ds(half, half), :] = f[:, per:]
-    for n in range(6):
-        all_bytes(recv.at[n], (n_row if n % 2 else n_col) - 1, esend.at[n]).wait()
-    all_bytes(rf, n_row - 1, gsend.at[0]).wait()
-    all_bytes(gf, n_col - 1, gsend.at[1]).wait()
+    all_bytes(recv.at[5], n_row - 1, esend.at[5]).wait()
 
 
 def body(n_row, n_col, gx, rx, w, b, wo):
@@ -446,10 +441,8 @@
             pltpu.VMEM((units, feat), BF16),
             pltpu.VMEM((n_col, per, feat), F32),
             pltpu.VMEM((n_row, per, feat), F32),
-            pltpu.VMEM((rows, feat), BF16),
-            pltpu.VMEM((rows, feat), BF16),
-            pltpu.VMEM((feat, cols), BF16),
-            pltpu.VMEM((feat, cols), BF16),
+            pltpu.VMEM((rows, 3 * feat), BF16),
+            pltpu.VMEM((3 * feat, cols), BF16),
             pltpu.VMEM((rows, cols), F32),
             pltpu.VMEM((rows, LANES), F32),
             pltpu.VMEM((rows, LANES), F32),

time: 61 us -> 59.9 us (0.982)
  Pallas kernels: 59.1 us -> 58 us
    pallas_call x1, Pallas kernels: 59.1 us -> 58 us  [body(): pl.pallas_call(functools.partial(kernel, n_row, n_col, math.isqrt(n_col))...]
where the time goes in v6:
time: 59.9 us; the launch traced here: 59.8 us
  Pallas kernels  58 us (97%)
  local copies, waits for them, and re-layouts  1.19 us (2%)
  between operations  0.64 us (1%)
    pallas_call x1, Pallas kernels, body(): pl.pallas_call(functools.partial(kernel, n_row, n_col, math.isqrt(n_col))...  58 us

profile of v6, /device:TPU:1, one launch (start us, length us, event | category | flops | bytes accessed | tf_op | source)
XLA Modules:
  0.0 59.8 jit_solution(5932256032471592541)
XLA Ops:
  0.6 58.0 %shard_map.68 = (f32[8,128]{1,0:T(8,128)S(1)}, f32[16,64]{1,0:T(8,128)S(1)}) custom-call(bf16[64,6480]{1,0:T(8,128)(2,1)} %gx.1, bf16[64,6480]{1,0:T(8,128)(2,1)} %rx.1, bf16[6480,512]{1,0:T(8,128)(2,1)} %w.1, f32[1,512]{1,0:T(1,128)} %bitcast.3, bf16[512,256]{1,0:T(8,128)(2,1)} %wo.1), custom_call_target="tpu_custom_call" | custom-call | tf_op jit(solution)/shard_map/pallas_call | solution.py:432
  58.6 0.6 copy.9
  59.2 0.6 copy.10

commit v7 on v6

--- a/solution.py
+++ b/solution.py
@@ -16,7 +16,7 @@
 K_CUTS = (2176, 4352)
 CHUNKS = 2
 RB = 32
-UNROLL = 8
+UNROLL = 16
 
 
 def split2(v):
@@ -140,7 +140,8 @@
     h1 = h1f.astype(BF16)
     h2 = (h1f - h1.astype(F32)).astype(BF16)
     wov = wo_v[...]
-    feats = mm(h0, wov) + (mm(h1, wov) + mm(h2, wov))
+    three = mm(jnp.concatenate([h0, h1, h2], axis=0), wov)
+    feats = three[: 2 * per] + (three[2 * per : 4 * per] + three[4 * per :])
     gf[my_c] = feats[:per]
     rf[my_r] = feats[per:]
 

time: 59.9 us -> 59.7 us (level)
  no operation moved by 1% of the time
where the time goes in v7:
time: 59.7 us; the launch traced here: 59.6 us
  Pallas kernels  57.7 us (97%)
  local copies, waits for them, and re-layouts  1.19 us (2%)
  between operations  0.64 us (1%)
    pallas_call x1, Pallas kernels, body(): pl.pallas_call(functools.partial(kernel, n_row, n_col, math.isqrt(n_col))...  57.7 us

profile of v7, /device:TPU:1, one launch (start us, length us, event | category | flops | bytes accessed | tf_op | source)
XLA Modules:
  0.0 59.6 jit_solution(11931358804341762692)
XLA Ops:
  0.6 57.7 %shard_map.68 = (f32[8,128]{1,0:T(8,128)S(1)}, f32[16,64]{1,0:T(8,128)S(1)}) custom-call(bf16[64,6480]{1,0:T(8,128)(2,1)} %gx.1, bf16[64,6480]{1,0:T(8,128)(2,1)} %rx.1, bf16[6480,512]{1,0:T(8,128)(2,1)} %w.1, f32[1,512]{1,0:T(1,128)} %bitcast.3, bf16[512,256]{1,0:T(8,128)(2,1)} %wo.1), custom_call_target="tpu_custom_call" | custom-call | tf_op jit(solution)/shard_map/pallas_call | solution.py:433
  58.4 0.6 copy.9
  59.0 0.6 %copy.10 = f32[16,64]{1,0:T(8,128)} copy(f32[16,64]{1,0:T(8,128)S(1)} %get-tuple-element.7) | data formatting | bytes 8192
